TPU v7x, 32 devices: a whole 2x2x4 slice. The times are simulated.
32 devices in a mesh: row: 4 (over z), replica: 4 (over y, core), feat: 2 (over x).
Axes of the slice: x: 2, y: 2, z: 4, core: 2. Of those that a mesh axis runs over, the one named last changes fastest.
Arguments:
- features: bfloat16 [4, 4096, 256], P('replica', ('row', 'feat')), may hold values from -6 to 6
- tiles: bfloat16 [4, 32, 4, 3, 128, 128], P('replica', ('row', 'feat')), may hold values from 0 to 1
- block_cols: int32 [4, 32, 4, 3], P('replica', ('row', 'feat')), may hold values from 0 to 7
- block_counts: int32 [4, 32, 4], P('replica', ('row', 'feat')), may hold values from 0 to 3, as said below
- degrees: int32 [4, 4096], P('replica', ('row', 'feat')), may hold values from 32 to 287
- w_self: bfloat16 [256, 256], P(None, 'feat'), may hold values from -0.375 to 0.375
- w_neigh: bfloat16 [256, 256], P(None, 'feat'), may hold values from -0.375 to 0.375
- gamma: float32 [256], P('feat'), may hold values from 0.5 to 1.5
- beta: float32 [256], P('feat'), may hold values from -3 to 3
Outputs:
- hidden_out: bfloat16 [4, 4096, 256], P('replica', 'row', 'feat')
Inputs may be any that keep to these rules, and one draw needn't show every extreme that they name: `block_counts`: some block row uses all 3 slots of some source shard in every partition.
All inputs are finite; a program needn't handle non-finite values.
Results may differ from a plain program's by a relative error of at most 0.001.
Values may be sent and summed in bfloat16 or wider, within the bound.
No kernel may reach another device: no remote copies, remote signals or barrier semaphores. Data moves between devices by JAX's collectives and lax.ppermute only.
A program may use at most 128 MiB of HBM per device.

v0:
```python
import jax
import jax.numpy as jnp
from jax import lax
from jax.sharding import PartitionSpec as P


def per_device(features, tiles, block_cols, block_counts, degrees, w_self, w_neigh, gamma, beta):
    local_x = features[0]
    local_tiles = tiles[0]
    local_cols = block_cols[0]
    local_counts = block_counts[0]
    nodes_here = local_x.shape[0]
    width = local_x.shape[1]
    block_size = local_tiles.shape[3]
    slots = local_tiles.shape[2]
    row_blocks = local_tiles.shape[0]
    pair = lax.all_gather(local_x, "feat", axis=0, tiled=True)
    shard_rows = pair.shape[0]
    shard_blocks = shard_rows // block_size
    slot_index = jnp.arange(slots, dtype=jnp.int32)[None, :]
    start_total = jnp.zeros((row_blocks, block_size, width), jnp.float32)
    piece = lax.all_gather(pair, "row", axis=0, tiled=True)
    count_shards = piece.shape[0] // shard_rows
    shards = piece.reshape(count_shards, shard_blocks, block_size, width)

    def one_shard(step, acc):
        shard = lax.dynamic_index_in_dim(shards, step, 0, keepdims=False)
        counts_now = lax.dynamic_index_in_dim(local_counts, step, 1, keepdims=False)
        cols_now = lax.dynamic_index_in_dim(local_cols, step, 1, keepdims=False)
        tiles_now = lax.dynamic_index_in_dim(local_tiles, step, 1, keepdims=False)
        picked = shard[cols_now]
        used = slot_index < counts_now[:, None]
        masked = jnp.where(used[:, :, None, None], tiles_now, jnp.zeros((), tiles_now.dtype))
        return acc + jnp.einsum(
            "bcij,bcjf->bif", masked, picked, preferred_element_type=jnp.float32
        )

    agg_sum = lax.fori_loop(0, count_shards, one_shard, start_total).reshape(nodes_here, width)
    agg = (agg_sum / degrees[0][:, None].astype(jnp.float32)).astype(jnp.bfloat16)
    agg_pair = lax.all_gather(agg, "feat", axis=0, tiled=True)
    pre = jnp.dot(pair, w_self, preferred_element_type=jnp.float32) + jnp.dot(
        agg_pair, w_neigh, preferred_element_type=jnp.float32
    )
    col_sum, col_sq = lax.psum(
        (jnp.sum(pre, axis=0), jnp.sum(pre * pre, axis=0)), ("row", "replica")
    )
    total_nodes = pre.shape[0] * lax.axis_size("row") * lax.axis_size("replica")
    mean = col_sum / total_nodes
    var = col_sq / total_nodes - mean * mean
    normed = gamma * (pre - mean) / jnp.sqrt(var + 1e-05) + beta
    return jnp.maximum(normed, 0.0).astype(jnp.bfloat16)[None]


def solution(mesh):
    in_specs = (
        P("replica", ("row", "feat"), None),
        P("replica", ("row", "feat"), None, None, None, None),
        P("replica", ("row", "feat"), None, None),
        P("replica", ("row", "feat"), None),
        P("replica", ("row", "feat")),
        P(None, "feat"),
        P(None, "feat"),
        P("feat"),
        P("feat"),
    )
    out_specs = P("replica", "row", "feat")
    return jax.shard_map(
        per_device, mesh=mesh, in_specs=in_specs, out_specs=out_specs, check_vma=False
    )
```

profile of v0, /device:TPU:0, one launch (start us, length us, event | category | flops | bytes accessed | tf_op | source)
XLA Modules:
  0.0 121.8 jit_solution(17375432722191585981)
XLA Ops:
  6.5 0.0 copy-start
  6.5 0.0 all-gather.4.cloned.1.call-start
  6.5 12.0 %all-gather = bf16[1,1024,256]{2,1,0:T(8,128)(2,1)} all-gather(bf16[1,512,256]{2,1,0:T(8,128)(2,1)} %param.11), channel_id=2, replica_groups=mesh['row'=4,'replica'=4,'feat'=2] {'feat'}, dimensions={1}, use_global_device_ids=true | all-gather | bytes 786432 | tf_op jit(solution)/shard_map/all_gather | solution.py:17
  18.6 0.0 all-gather.4.cloned.1.call-update
  18.6 0.0 copy-start.4
  18.6 0.0 copy-start.5
  18.6 0.0 copy-start.6
  18.6 0.0 copy-start.1
  18.7 0.0 copy-start.3
  18.7 1.6 %copy.20 = bf16[1,4,4,3,128,128]{5,4,3,1,2,0:T(8,128)(2,1)S(1)} copy(bf16[1,4,4,3,128,128]{5,4,3,2,1,0:T(8,128)(2,1)} %param.12) | data formatting | bytes 3145728 | tf_op args[1]
  20.2 0.0 copy-done.4
  20.3 0.1 copy.17
  20.4 0.0 copy-done.5
  20.4 0.1 copy.16
  20.5 1.1 fusion.10
  21.6 43.2 %all-gather.4.cloned.1.call-done = bf16[1,4096,256]{2,1,0:T(8,128)(2,1)} async-done(((bf16[1,1024,256]{2,1,0:T(8,128)(2,1)}), bf16[1,4096,256]{2,1,0:T(8,128)(2,1)}) %all-gather.4.cloned.1.call-update) | async-done | bytes 2097168 | tf_op jit(solution)/shard_map/all_gather | solution.py:22
  64.7 9.8 %while.14 = (s32[]{:T(128)}, f32[4,128,256]{2,1,0:T(8,128)S(1)}, s32[4,4]{0,1:T(4,128)S(1)}, bf16[4,4,3,128,128]{4,3,2,0,1:T(8,128)(2,1)S(1)}, bf16[4,8,128,256]...) while((s32[]{:T(128)}, f32[4,128,256]{2,1,0:T(8,128)S(1)}, ...), condition=%wide.region_1.2_spmd.clone, body=%wide.region_0.1_spmd.clone.sunk | while | flops 101123120 | bytes 4854827 | solution.py:38
  64.7 1.1 dynamic-slice_bitcast_fusion.2
  65.8 0.1 copy.22
  65.9 0.1 reshape.106
  66.0 0.6 gather_fusion
  66.6 0.1 iota_compare_fusion.2
  66.7 0.4 fusion.23
  67.2 1.1 dynamic-slice_bitcast_fusion.2
  68.3 0.1 copy.22
  68.4 0.1 reshape.106
  68.5 0.6 gather_fusion
  69.1 0.1 iota_compare_fusion.2
  69.2 0.4 fusion.23
  69.6 1.1 dynamic-slice_bitcast_fusion.2
  70.7 0.1 copy.22
  70.8 0.1 reshape.106
  70.9 0.6 gather_fusion
  71.5 0.1 iota_compare_fusion.2
  71.6 0.4 fusion.23
  72.1 1.1 dynamic-slice_bitcast_fusion.2
  73.2 0.1 copy.22
  73.2 0.1 reshape.106
  73.3 0.6 gather_fusion
  74.0 0.1 iota_compare_fusion.2
  74.0 0.4 fusion.23
  74.5 0.0 copy-start.7
  74.5 0.0 copy-start.8
  74.5 0.1 fusion.9
  74.7 8.6 %all_gather.11 = bf16[1024,256]{1,0:T(8,128)(2,1)S(1)} all-gather(bf16[512,256]{1,0:T(8,128)(2,1)S(1)} %fusion.9), channel_id=1, replica_groups=mesh['row'=4,'replica'=4,'feat'=2] {'feat'}, dimensions={0}, use_global_device_ids=true | all-gather | bytes 786432 | tf_op jit(solution)/shard_map/all_gather | solution.py:40
  83.2 0.4 fusion.13
  83.6 30.5 %all-reduce = (f32[128]{0:T(128)S(1)}, f32[128]{0:T(128)S(1)}) all-reduce(f32[128]{0:T(128)S(1)} %get-tuple-element.166, f32[128]{0:T(128)S(1)} %get-tuple-element.165), channel_id=1, replica_groups=mesh['row'=4,'replica'=4,'feat'=2] {'row','replica'}, use_global_device_ids=true, to_apply=%region_5.6 | all-reduce | flops 256 | bytes 2048 | tf_op jit(solution)/shard_map/psum | solution.py:44
  114.2 0.8 fusion.12
  (23 shorter events, 0.2 us)
Async XLA Ops:
  6.5 76.7 %copy-start = (bf16[256,128]{1,0:T(8,128)(2,1)S(1)}, bf16[256,128]{1,0:T(8,128)(2,1)}, u32[]{:S(2)}) copy-start(bf16[256,128]{1,0:T(8,128)(2,1)} %param.17) | copy-start | bytes 196612
  6.5 58.2 %all-gather.4.cloned.1.call-start = ((), (), s32[]{:S(2)}) async-start(), calls=%async_computation | async-start | bytes 2621440 | tf_op jit(solution)/shard_map/all_gather | solution.py:22
  18.6 1.6 %copy-start.4 = (s32[1,4,4,3]{2,1,3,0:T(4,128)S(1)}, s32[1,4,4,3]{2,1,3,0:T(4,128)}, u32[]{:S(2)}) copy-start(s32[1,4,4,3]{2,1,3,0:T(4,128)} %param.13) | copy-start | bytes 580
  18.6 1.7 %copy-start.5 = (s32[1,4,4]{2,1,0:T(4,128)S(1)}, s32[1,4,4]{2,1,0:T(4,128)}, u32[]{:S(2)}) copy-start(s32[1,4,4]{2,1,0:T(4,128)} %param.14) | copy-start | bytes 196
  18.6 1.8 %copy-start.6 = (s32[1,512]{1,0:T(1,128)S(1)}, s32[1,512]{1,0:T(1,128)}, u32[]{:S(2)}) copy-start(s32[1,512]{1,0:T(1,128)} %param.15) | copy-start | bytes 6148
  18.6 1.8 %copy-start.1 = (bf16[1,1024,256]{2,1,0:T(8,128)(2,1)S(1)}, bf16[1,1024,256]{2,1,0:T(8,128)(2,1)}, u32[]{:S(2)}) copy-start(bf16[1,1024,256]{2,1,0:T(8,128)(2,1)} %all-gather) | copy-start | bytes 1572868
  18.7 1.8 %copy-start.3 = (bf16[256,128]{1,0:T(8,128)(2,1)S(1)}, bf16[256,128]{1,0:T(8,128)(2,1)}, u32[]{:S(2)}) copy-start(bf16[256,128]{1,0:T(8,128)(2,1)} %param.16) | copy-start | bytes 196612
  74.5 8.7 %copy-start.2 = (f32[1024,128]{1,0:T(8,128)S(1)}, f32[1024,128]{1,0:T(8,128)}, u32[]{:S(2)}) copy-start(f32[1024,128]{1,0:T(8,128)} %fusion.10) | copy-start | bytes 1572868
  74.5 39.7 %copy-start.7 = (f32[128]{0:T(128)S(1)}, f32[128]{0:T(128)}, u32[]{:S(2)}) copy-start(f32[128]{0:T(128)} %param.19) | copy-start | bytes 1540
  74.5 39.7 %copy-start.8 = (f32[128]{0:T(128)S(1)}, f32[128]{0:T(128)}, u32[]{:S(2)}) copy-start(f32[128]{0:T(128)} %param.18) | copy-start | bytes 1540
Sparse Core Ops, SparseCore 0:
  18.7 45.9 all-gather.3
where the time goes:
time: 122 us
  blocking collectives  51.1 us (42%)
  waiting for transfers between devices  43.2 us (35%)
  between operations  13.5 us (11%)
  local copies, waits for them, and re-layouts  9.28 us (8%)
  matrix products  3.2 us (3%)
  other arithmetic  1.35 us (1%)
    all_gather x1, waiting for transfers between devices, per_device(): piece = lax.all_gather(pair, 'row', axis=0, tiled=True)  43.2 us
    psum x1, blocking collectives, per_device(): lax.psum((jnp.sum(pre, axis=0), jnp.sum(pre * pre, axis=0)), ('row', 'rep...  30.5 us
    all_gather x1, blocking collectives, per_device(): pair = lax.all_gather(local_x, 'feat', axis=0, tiled=True)  12 us
    all_gather x1, blocking collectives, per_device(): agg_pair = lax.all_gather(agg, 'feat', axis=0, tiled=True)  8.55 us
    squeeze x4, local copies, waits for them, and re-layouts, one_shard(): shard = lax.dynamic_index_in_dim(shards, step, 0, keepdims=False)  4.32 us
  transfers between devices with their start and end apart: 1, of which 1 were waited for; matrix products, arithmetic and copies ran while one was open for 2% of the time, Pallas kernels for 0%

commit v1 on v0

--- a/solution.py
+++ b/solution.py
@@ -2,6 +2,12 @@
 import jax.numpy as jnp
 from jax import lax
 from jax.sharding import PartitionSpec as P
+
+
+def supply_plane(xs, axis_k):
+    low = list(xs.shape[1:])
+    low[axis_k] *= xs.shape[0]
+    return jnp.moveaxis(xs, 0, axis_k).reshape(low)
 
 
 def per_device(features, tiles, block_cols, block_counts, degrees, w_self, w_neigh, gamma, beta):
@@ -19,7 +25,14 @@
     shard_blocks = shard_rows // block_size
     slot_index = jnp.arange(slots, dtype=jnp.int32)[None, :]
     start_total = jnp.zeros((row_blocks, block_size, width), jnp.float32)
-    piece = lax.all_gather(pair, "row", axis=0, tiled=True)
+    p_count = jax.lax.axis_size("row")
+    pile = [pair]
+    windows = [(h, (h + 1) % p_count) for h in range(p_count)]
+    while len(pile) < p_count:
+        pile.append(jax.lax.ppermute(pile[-1], axis_name="row", perm=windows))
+    before = jax.lax.axis_index("row")
+    pile = jnp.stack(pile, axis=0)[(before - jnp.arange(p_count)) % p_count]
+    piece = supply_plane(pile, 0)
     count_shards = piece.shape[0] // shard_rows
     shards = piece.reshape(count_shards, shard_blocks, block_size, width)
 

time: 122 us -> 109 us (0.89)
  between operations: 13.5 us -> 0.09 us
  waiting for transfers between devices: 43.2 us -> 36 us
  local copies, waits for them, and re-layouts: 9.28 us -> 13.5 us
  blocking collectives: 51.1 us -> 46.9 us
  matrix products: 3.2 us -> 7.18 us
  starting transfers between devices: 0.01 us -> 1.78 us
  other arithmetic: 1.35 us -> 2.99 us
    all_gather x1 -> x0, waiting for transfers between devices: 43.2 us -> none  [per_device(): piece = lax.all_gather(pair, 'row', axis=0, tiled=True)]
    ppermute x0 -> x3, waiting for transfers between devices: none -> 36 us  [per_device(): pile.append(jax.lax.ppermute(pile[-1], axis_name='row', perm=windows))]
    dot_general x4, matrix products: 1.73 us -> 5.71 us  [one_shard(): jnp.einsum('bcij,bcjf->bif', masked, picked, preferred_element_type=jnp.f...]
    unnamed x21 -> x25, local copies, waits for them, and re-layouts: 1.82 us -> 3.99 us
    gather x0 -> x1, local copies, waits for them, and re-layouts: none -> 2.02 us  [per_device(): pile = jnp.stack(pile, axis=0)[(before - jnp.arange(p_count)) % p_count]]
    ppermute x0 -> x3, starting transfers between devices: none -> 1.78 us  [per_device(): pile.append(jax.lax.ppermute(pile[-1], axis_name='row', perm=windows))]
    all_gather x1, blocking collectives: 12 us -> 10.3 us  [per_device(): pair = lax.all_gather(local_x, 'feat', axis=0, tiled=True)]
    another operation x0 -> x1, other arithmetic: none -> 1.62 us  [per_device(): pile = jnp.stack(pile, axis=0)[(before - jnp.arange(p_count)) % p_count]]
  transfers between devices with their start and end apart: 1 -> 3, of which waited for: 1 -> 3; matrix products, arithmetic and copies ran while one was open for 2% -> 4% of each run, Pallas kernels for 0% -> 0%
where the time goes in v1:
time: 109 us
  blocking collectives  46.9 us (43%)
  waiting for transfers between devices  36 us (33%)
  local copies, waits for them, and re-layouts  13.5 us (12%)
  matrix products  7.18 us (7%)
  other arithmetic  2.99 us (3%)
  starting transfers between devices  1.78 us (2%)
    ppermute x3, waiting for transfers between devices, per_device(): pile.append(jax.lax.ppermute(pile[-1], axis_name='row', perm=windows))  36 us
    psum x1, blocking collectives, per_device(): lax.psum((jnp.sum(pre, axis=0), jnp.sum(pre * pre, axis=0)), ('row', 'rep...  29.5 us
    all_gather x1, blocking collectives, per_device(): pair = lax.all_gather(local_x, 'feat', axis=0, tiled=True)  10.3 us
    all_gather x1, blocking collectives, per_device(): agg_pair = lax.all_gather(agg, 'feat', axis=0, tiled=True)  7.04 us
    dot_general x4, matrix products, one_shard(): jnp.einsum('bcij,bcjf->bif', masked, picked, preferred_element_type=jnp.f...  5.71 us
    squeeze x4, local copies, waits for them, and re-layouts, one_shard(): shard = lax.dynamic_index_in_dim(shards, step, 0, keepdims=False)  4.37 us
    unnamed x25, local copies, waits for them, and re-layouts  3.99 us
    gather x4, local copies, waits for them, and re-layouts, one_shard(): picked = shard[cols_now]  2.39 us
  transfers between devices with their start and end apart: 3, of which 3 were waited for; matrix products, arithmetic and copies ran while one was open for 4% of the time, Pallas kernels for 0%

profile of v1, /device:TPU:0, one launch (start us, length us, event | category | flops | bytes accessed | tf_op | source)
XLA Modules:
  0.0 108.7 jit_solution(16725656005644445213)
XLA Ops:
  0.0 0.0 copy-start
  0.0 0.0 copy-start.5
  0.0 10.3 %all-gather = bf16[1,1024,256]{2,1,0:T(8,128)(2,1)S(1)} all-gather(bf16[1,512,256]{2,1,0:T(8,128)(2,1)} %param.11), channel_id=2, replica_groups=mesh['row'=4,'replica'=4,'feat'=2] {'feat'}, dimensions={1}, use_global_device_ids=true | all-gather | bytes 786432 | tf_op jit(solution)/shard_map/all_gather | solution.py:23
  10.4 1.8 %collective-permute-start = (bf16[1024,256]{1,0:T(8,128)(2,1)S(1)}, bf16[1024,256]{1,0:T(8,128)(2,1)S(1)}, u32[]{:S(2)}, u32[]{:S(2)}) collective-permute-start(bf16[1024,256]{1,0:T(8,128)(2,1)S(1)} %bitcast.59), channel_id=1, source_target_pairs={{0,8},{8,16},{16,24},{24,0},{1,9},{9,17},{17,25},{25,1},{2,10},{10... | collective-permute-start | bytes 1572872 | tf_op jit(solution)/shard_map/ppermute | solution.py:32
  12.1 13.1 %collective-permute-done = bf16[1024,256]{1,0:T(8,128)(2,1)S(1)} collective-permute-done((bf16[1024,256]{1,0:T(8,128)(2,1)S(1)}, bf16[1024,256]{1,0:T(8,128)(2,1)S(1)}, u32[]{:S(2)}, u32[]{:S(2)}) %collective-permute-start) | collective-permute-done | bytes 524320 | tf_op jit(solution)/shard_map/ppermute | solution.py:32
  25.3 0.0 collective-permute-start.1
  25.3 14.0 %collective-permute-done.1 = bf16[1024,256]{1,0:T(8,128)(2,1)S(1)} collective-permute-done((bf16[1024,256]{1,0:T(8,128)(2,1)S(1)}, bf16[1024,256]{1,0:T(8,128)(2,1)S(1)}, u32[]{:S(2)}, u32[]{:S(2)}) %collective-permute-start.1) | collective-permute-done | bytes 524320 | tf_op jit(solution)/shard_map/ppermute | solution.py:32
  39.3 0.0 collective-permute-start.2
  39.3 2.9 %copy.20 = bf16[1,4,4,3,128,128]{5,4,3,1,2,0:T(8,128)(2,1)} copy(bf16[1,4,4,3,128,128]{5,4,3,2,1,0:T(8,128)(2,1)} %param.12) | data formatting | bytes 3145728 | tf_op args[1]
  42.2 0.1 copy.17
  42.3 0.1 copy.16
  42.5 1.1 %fusion.13 = f32[1024,128]{1,0:T(8,128)} fusion(bf16[256,128]{1,0:T(8,128)(2,1)S(1)} %copy-done.5, bf16[1,1024,256]{2,1,0:T(8,128)(2,1)S(1)} %all-gather), kind=kOutput, calls=%fused_computation.34 | convolution fusion | flops 67108864 | bytes 1114112 | tf_op jit(solution)/shard_map/dot_general | solution.py:54
  43.6 8.9 %collective-permute-done.2 = bf16[1024,256]{1,0:T(8,128)(2,1)S(1)} collective-permute-done((bf16[1024,256]{1,0:T(8,128)(2,1)S(1)}, bf16[1024,256]{1,0:T(8,128)(2,1)S(1)}, u32[]{:S(2)}, u32[]{:S(2)}) %collective-permute-start.2) | collective-permute-done | bytes 524320 | tf_op jit(solution)/shard_map/ppermute | solution.py:32
  52.5 0.8 copy-done.4
  53.3 1.6 %pad_maximum_fusion = bf16[4,1024,256]{2,1,0:T(8,128)(2,1)S(1)} fusion(bf16[1,1024,256]{2,1,0:T(8,128)(2,1)} %bitcast.62, bf16[1,1024,256]{2,1,0:T(8,128)(2,1)} %bitcast.61, bf16[1,1024,256]{2,1,0:T(8,128)(2,1)} %bitcast.60, bf16[1,1024,256]{2,1,0:T(8,128)(2,1)S(1)} %all-gather), kind=kLoop, calls=%fused_computation.17 | loop fusion | flops 3145728 | bytes 4194304 | tf_op jit(solution)/shard_map/stack | solution.py:34
  54.9 2.0 %gather_fusion.1 = bf16[4,1024,256]{2,1,0:T(8,128)(2,1)} fusion(bf16[4,1024,256]{2,1,0:T(8,128)(2,1)S(1)} %pad_maximum_fusion, s32[1024]{0:T(1024)S(1)} %pad_clamp_fusion.1), kind=kCustom, calls=%fused_computation.1 | custom fusion | bytes 4194320 | tf_op jit(solution)/shard_map/gather | solution.py:34
  56.9 13.8 %while.14 = (s32[]{:T(128)}, f32[4,128,256]{2,1,0:T(8,128)S(1)}, s32[4,4]{0,1:T(4,128)S(1)}, bf16[4,4,3,128,128]{4,3,2,0,1:T(8,128)(2,1)}, bf16[4,8,128,256]{3,2...) while((s32[]{:T(128)}, f32[4,128,256]{2,1,0:T(8,128)S(1)}, ...), condition=%wide.region_1.2_spmd.clone, body=%wide.region_0.1_spmd.clone.sunk | while | flops 101123120 | bytes 4854835 | solution.py:51
  56.9 1.1 %dynamic-slice_bitcast_fusion.2 = bf16[8,128,256]{2,1,0:T(8,128)(2,1)S(1)} fusion(bf16[4,8,128,256]{3,2,1,0:T(8,128)(2,1)} %get-tuple-element.241, s32[]{:T(128)} %get-tuple-element.229), kind=kLoop, calls=%fused_computation.5.clone.1 | loop fusion | bytes 1048580 | tf_op jit(solution)/shard_map/while/body/eval_jaxpr/jit(dynamic_index_in_dim)/squeeze | solution.py:40
  58.1 0.1 copy.22
  58.2 0.1 reshape.158
  58.3 0.6 gather_fusion
  58.9 0.1 iota_compare_fusion.2
  59.0 1.4 %fusion.25 = f32[4,128,256]{2,1,0:T(8,128)S(1)} fusion(bf16[4,3,128,256]{3,2,1,0:T(8,128)(2,1)S(1)} %bitcast.56, f32[4,128,256]{2,1,0:T(8,128)S(1)} %get-tuple-element.230, bf16[4,4,3,128,128]{4,3,2,0,1:T(8,128)(2,1)} %get-tuple-element.240, s32[]{:T(128)} %get-tuple-element.229, pred[4,3]{1,0:T(4,128)(4,1)S(1)} %iota_compare_fusion.2, pred[]{:T(512)S(6)} %compare.10), kind=kOutput, calls=%fused_computation.4.clone.1 | convolution fusion | flops 101122048 | bytes 2228749 | tf_op jit(solution)/shard_map/while/body/eval_jaxpr/bcij,bcjf->bif/dot_general | solution.py:47
  60.4 1.1 dynamic-slice_bitcast_fusion.2
  61.5 0.1 copy.22
  61.6 0.1 reshape.158
  61.7 0.6 gather_fusion
  62.3 0.1 iota_compare_fusion.2
  62.4 1.4 %fusion.25 = f32[4,128,256]{2,1,0:T(8,128)S(1)} fusion(bf16[4,3,128,256]{3,2,1,0:T(8,128)(2,1)S(1)} %bitcast.56, f32[4,128,256]{2,1,0:T(8,128)S(1)} %get-tuple-element.230, bf16[4,4,3,128,128]{4,3,2,0,1:T(8,128)(2,1)} %get-tuple-element.240, s32[]{:T(128)} %get-tuple-element.229, pred[4,3]{1,0:T(4,128)(4,1)S(1)} %iota_compare_fusion.2, pred[]{:T(512)S(6)} %compare.10), kind=kOutput, calls=%fused_computation.4.clone.1 | convolution fusion | flops 101122048 | bytes 2228749 | tf_op jit(solution)/shard_map/while/body/eval_jaxpr/bcij,bcjf->bif/dot_general | solution.py:47
  63.9 1.1 dynamic-slice_bitcast_fusion.2
  65.0 0.1 copy.22
  65.1 0.1 reshape.158
  65.1 0.6 gather_fusion
  65.8 0.1 iota_compare_fusion.2
  65.8 1.4 %fusion.25 = f32[4,128,256]{2,1,0:T(8,128)S(1)} fusion(bf16[4,3,128,256]{3,2,1,0:T(8,128)(2,1)S(1)} %bitcast.56, f32[4,128,256]{2,1,0:T(8,128)S(1)} %get-tuple-element.230, bf16[4,4,3,128,128]{4,3,2,0,1:T(8,128)(2,1)} %get-tuple-element.240, s32[]{:T(128)} %get-tuple-element.229, pred[4,3]{1,0:T(4,128)(4,1)S(1)} %iota_compare_fusion.2, pred[]{:T(512)S(6)} %compare.10), kind=kOutput, calls=%fused_computation.4.clone.1 | convolution fusion | flops 101122048 | bytes 2228749 | tf_op jit(solution)/shard_map/while/body/eval_jaxpr/bcij,bcjf->bif/dot_general | solution.py:47
  67.3 1.1 dynamic-slice_bitcast_fusion.2
  68.4 0.1 copy.22
  68.5 0.1 reshape.158
  68.6 0.6 gather_fusion
  69.2 0.1 iota_compare_fusion.2
  69.3 1.4 %fusion.25 = f32[4,128,256]{2,1,0:T(8,128)S(1)} fusion(bf16[4,3,128,256]{3,2,1,0:T(8,128)(2,1)S(1)} %bitcast.56, f32[4,128,256]{2,1,0:T(8,128)S(1)} %get-tuple-element.230, bf16[4,4,3,128,128]{4,3,2,0,1:T(8,128)(2,1)} %get-tuple-element.240, s32[]{:T(128)} %get-tuple-element.229, pred[4,3]{1,0:T(4,128)(4,1)S(1)} %iota_compare_fusion.2, pred[]{:T(512)S(6)} %compare.10), kind=kOutput, calls=%fused_computation.4.clone.1 | convolution fusion | flops 101122048 | bytes 2228749 | tf_op jit(solution)/shard_map/while/body/eval_jaxpr/bcij,bcjf->bif/dot_general | solution.py:47
  70.7 0.0 copy-start.9
  70.7 0.0 copy-start.10
  70.7 0.1 fusion.9
  70.9 7.0 %all_gather.7 = bf16[1024,256]{1,0:T(8,128)(2,1)S(1)} all-gather(bf16[512,256]{1,0:T(8,128)(2,1)S(1)} %fusion.9), channel_id=1, replica_groups=mesh['row'=4,'replica'=4,'feat'=2] {'feat'}, dimensions={0}, use_global_device_ids=true | all-gather | bytes 786432 | tf_op jit(solution)/shard_map/all_gather | solution.py:53
  77.9 0.4 fusion.15
  78.3 29.5 %all-reduce = (f32[128]{0:T(128)S(1)}, f32[128]{0:T(128)S(1)}) all-reduce(f32[128]{0:T(128)S(1)} %get-tuple-element.166, f32[128]{0:T(128)S(1)} %get-tuple-element.165), channel_id=1, replica_groups=mesh['row'=4,'replica'=4,'feat'=2] {'row','replica'}, use_global_device_ids=true, to_apply=%region_5.6 | all-reduce | flops 256 | bytes 2048 | tf_op jit(solution)/shard_map/psum | solution.py:57
  107.8 0.8 fusion.10
  (34 shorter events, 0.2 us)
Async XLA Ops:
  0.0 77.9 %copy-start = (bf16[256,128]{1,0:T(8,128)(2,1)S(1)}, bf16[256,128]{1,0:T(8,128)(2,1)}, u32[]{:S(2)}) copy-start(bf16[256,128]{1,0:T(8,128)(2,1)} %param.17) | copy-start | bytes 196612
  0.0 42.2 %copy-start.6 = (s32[1,4,4,3]{2,1,3,0:T(4,128)S(1)}, s32[1,4,4,3]{2,1,3,0:T(4,128)}, u32[]{:S(2)}) copy-start(s32[1,4,4,3]{2,1,3,0:T(4,128)} %param.13) | copy-start | bytes 580
  0.0 42.3 %copy-start.7 = (s32[1,4,4]{2,1,0:T(4,128)S(1)}, s32[1,4,4]{2,1,0:T(4,128)}, u32[]{:S(2)}) copy-start(s32[1,4,4]{2,1,0:T(4,128)} %param.14) | copy-start | bytes 196
  0.0 42.4 %copy-start.8 = (s32[1,512]{1,0:T(1,128)S(1)}, s32[1,512]{1,0:T(1,128)}, u32[]{:S(2)}) copy-start(s32[1,512]{1,0:T(1,128)} %param.15) | copy-start | bytes 6148
  0.0 42.4 %copy-start.5 = (bf16[256,128]{1,0:T(8,128)(2,1)S(1)}, bf16[256,128]{1,0:T(8,128)(2,1)}, u32[]{:S(2)}) copy-start(bf16[256,128]{1,0:T(8,128)(2,1)} %param.16) | copy-start | bytes 196612
  10.4 14.9 %collective-permute-start = (bf16[1024,256]{1,0:T(8,128)(2,1)S(1)}, bf16[1024,256]{1,0:T(8,128)(2,1)S(1)}, u32[]{:S(2)}, u32[]{:S(2)}) collective-permute-start(bf16[1024,256]{1,0:T(8,128)(2,1)S(1)} %bitcast.59), channel_id=1, source_target_pairs={{0,8},{8,16},{16,24},{24,0},{1,9},{9,17},{17,25},{25,1},{2,10},{10... | collective-permute-start | bytes 1572872 | tf_op jit(solution)/shard_map/ppermute | solution.py:32
  25.3 18.3 %copy-start.2 = (bf16[1024,256]{1,0:T(8,128)(2,1)}, bf16[1024,256]{1,0:T(8,128)(2,1)S(1)}, u32[]{:S(2)}) copy-start(bf16[1024,256]{1,0:T(8,128)(2,1)S(1)} %collective-permute-done) | copy-start | bytes 1572868
  25.3 14.0 %collective-permute-start.1 = (bf16[1024,256]{1,0:T(8,128)(2,1)S(1)}, bf16[1024,256]{1,0:T(8,128)(2,1)S(1)}, u32[]{:S(2)}, u32[]{:S(2)}) collective-permute-start(bf16[1024,256]{1,0:T(8,128)(2,1)S(1)} %collective-permute-done), channel_id=1, source_target_pairs={{0,8},{8,16},{16,24},{24,0},{1,9},{9,17},{17,25},{25,1},{2,10},{10... | collective-permute-start | bytes 1572872 | tf_op jit(solution)/shard_map/ppermute | solution.py:32
  39.3 4.3 %copy-start.3 = (bf16[1024,256]{1,0:T(8,128)(2,1)}, bf16[1024,256]{1,0:T(8,128)(2,1)S(1)}, u32[]{:S(2)}) copy-start(bf16[1024,256]{1,0:T(8,128)(2,1)S(1)} %collective-permute-done.1) | copy-start | bytes 1572868
  39.3 13.2 %collective-permute-start.2 = (bf16[1024,256]{1,0:T(8,128)(2,1)S(1)}, bf16[1024,256]{1,0:T(8,128)(2,1)S(1)}, u32[]{:S(2)}, u32[]{:S(2)}) collective-permute-start(bf16[1024,256]{1,0:T(8,128)(2,1)S(1)} %collective-permute-done.1), channel_id=1, source_target_pairs={{0,8},{8,16},{16,24},{24,0},{1,9},{9,17},{17,25},{25,1},{2,10},{10... | collective-permute-start | bytes 1572872 | tf_op jit(solution)/shard_map/ppermute | solution.py:32
  52.5 0.8 copy-start.4
  56.9 21.0 %copy-start.1 = (f32[1024,128]{1,0:T(8,128)S(1)}, f32[1024,128]{1,0:T(8,128)}, u32[]{:S(2)}) copy-start(f32[1024,128]{1,0:T(8,128)} %fusion.13) | copy-start | bytes 1572868
  70.7 37.1 %copy-start.9 = (f32[128]{0:T(128)S(1)}, f32[128]{0:T(128)}, u32[]{:S(2)}) copy-start(f32[128]{0:T(128)} %param.19) | copy-start | bytes 1540
  70.7 37.1 %copy-start.10 = (f32[128]{0:T(128)S(1)}, f32[128]{0:T(128)}, u32[]{:S(2)}) copy-start(f32[128]{0:T(128)} %param.18) | copy-start | bytes 1540
